TPU v7x, 32 devices: a whole 2x2x4 slice. The times are simulated.
32 devices in a mesh: scene: 8 (over z, y), image: 4 (over x, core).
Axes of the slice: x: 2, y: 2, z: 4, core: 2. Of those that a mesh axis runs over, the one named last changes fastest.
Arguments:
- jacobian: bfloat16 [256, 256, 1152], P(('scene', 'image')), may hold values from -0.1875 to 0.1875
- splat_ids: int32 [256, 128], P(('scene', 'image')), may hold values from 0 to 8191, as said below
- pix_residual: bfloat16 [256, 256], P(('scene', 'image')), may hold values from -6 to 6
- live_blocks: int32 [32], replicated, may hold values from 1 to 8, as said below
- proj_jac: bfloat16 [9, 59, 8192], P(None, None, 'scene'), may hold values from -0.75 to 0.75
- damping: float32 [59, 8192], P(None, 'scene'), may hold values from 0.1 to 1
- precond: float32 [59, 8192], P(None, 'scene'), may hold values from 0.3 to 9
Outputs:
- solution: float32 [59, 8192], P(None, 'scene')
- residual: float32 [59, 8192], P(None, 'scene')
Inputs may be any that keep to these rules, and one draw needn't show every extreme that they name: live_blocks[d] counts the blocks in use on device d = scene index * 4 + image index; they are its slots 0 to live_blocks[d] - 1; some device uses all 8 while the device whose index differs from it in the lowest bit uses at most half of them. `splat_ids`: splat s of every block names a Gaussian of scene index s // 16, that is an id from that index times 1024 to the next such multiple.
All inputs are finite; a program needn't handle non-finite values.
Results may differ from a plain program's by a relative error of at most 0.0051.
Values may be sent and summed in bfloat16 or wider, within the bound.
A program may use at most 64 MiB of HBM per device.

v0:
```python
import jax
import jax.numpy as jnp
from jax import lax
from jax.sharding import PartitionSpec as P

ITERS = 2


def project(proj_jac, field):
    return jnp.einsum(
        "kag,ag->kg", proj_jac.astype(jnp.float32), field, precision=lax.Precision.HIGHEST
    ).astype(jnp.bfloat16)


def lift(proj_jac, weights):
    return jnp.einsum(
        "kag,kg->ag", proj_jac.astype(jnp.float32), weights, precision=lax.Precision.HIGHEST
    )


def run_blocks(jac_set, pixel_set, first_pos, last_pos, picker, keeper, initial):

    def advance(position, running):
        jac_block = lax.dynamic_index_in_dim(jac_set, position, 0, keepdims=False)
        if picker is None:
            signal = lax.dynamic_index_in_dim(pixel_set, position, 0, keepdims=False)
        else:
            signal = jnp.dot(
                jac_block, picker(position), preferred_element_type=jnp.float32
            ).astype(jnp.bfloat16)
        returned = jnp.dot(signal, jac_block, preferred_element_type=jnp.float32)
        return keeper(running, position, returned)

    return lax.fori_loop(first_pos, last_pos, advance, initial)


def local(jacobian, splat_ids, pix_residual, live_blocks, proj_jac, damping, precond):
    g_dev = damping.shape[1]
    n_proj = proj_jac.shape[0]
    n_scene = lax.axis_size("scene")
    owner_width = splat_ids.shape[1] // n_scene
    scene_pos = lax.axis_index("scene")
    device_pos = scene_pos * lax.axis_size("image") + lax.axis_index("image")
    own_live = live_blocks[device_pos]
    block_sets = [(jacobian, splat_ids, pix_residual, 0, own_live)]
    offsets = []
    total_slots = 0
    member = block_sets[0]
    offsets.append(total_slots)
    total_slots += member[0].shape[0]
    ids_all = jnp.concatenate([member[1] for member in block_sets], axis=0)
    routed_ids = lax.all_to_all(
        ids_all.reshape(total_slots, n_scene, owner_width),
        "scene",
        split_axis=1,
        concat_axis=1,
        tiled=True,
    )
    local_ids = routed_ids - scene_pos * g_dev

    def back_project(source):
        buffer = jnp.zeros((total_slots, n_proj, n_scene, owner_width), jnp.float32)
        for index_set, (jac_set, id_set, pixel_set, first_pos, last_pos) in enumerate(block_sets):
            slot_base = offsets[index_set]

            def keeper(running, position, returned):
                shaped = returned.reshape(n_proj, n_scene, owner_width)
                return lax.dynamic_update_index_in_dim(running, shaped, slot_base + position, 0)

            picker = (
                None
                if source is None
                else lambda position: lax.dynamic_index_in_dim(
                    source, slot_base + position, 0, keepdims=False
                )
            )
            buffer = run_blocks(jac_set, pixel_set, first_pos, last_pos, picker, keeper, buffer)
        arrived = lax.all_to_all(buffer, "scene", split_axis=2, concat_axis=2, tiled=True)
        arrivals = jnp.moveaxis(arrived, 1, 0).reshape(n_proj, -1)
        partial_sum = (
            jnp.zeros((n_proj, g_dev), jnp.float32).at[:, local_ids.reshape(-1)].add(arrivals)
        )
        return lax.psum(partial_sum, "image")

    def norm_dot(residual, precon_res):
        return lax.psum(jnp.sum(residual * precon_res), "scene")

    residual = -lift(proj_jac, back_project(None))
    solution = jnp.zeros_like(residual)
    precon_res = precond * residual
    direction = precon_res
    rz_now = norm_dot(residual, precon_res)
    for iteration in range(ITERS):
        local_proj = project(proj_jac, direction)
        picked = jnp.moveaxis(jnp.take(local_proj, local_ids, axis=1), 0, 1)
        fetched = lax.all_to_all(picked, "scene", split_axis=2, concat_axis=2, tiled=True).reshape(
            total_slots, -1
        )
        image = lift(proj_jac, back_project(fetched)) + damping * direction
        alpha = rz_now / lax.psum(jnp.sum(direction * image), "scene")
        solution = solution + alpha * direction
        residual = residual - alpha * image
        precon_res = precond * residual
        rz_next = norm_dot(residual, precon_res)
        direction = precon_res + rz_next / rz_now * direction
        rz_now = rz_next
    return (solution, residual)


def solution(mesh):
    return jax.shard_map(
        local,
        mesh=mesh,
        in_specs=(
            P(("scene", "image"), None, None),
            P(("scene", "image"), None),
            P(("scene", "image"), None),
            P(),
            P(None, None, "scene"),
            P(None, "scene"),
            P(None, "scene"),
        ),
        out_specs=(P(None, "scene"), P(None, "scene")),
        check_vma=False,
    )
```

profile of v0, /device:TPU:0, one launch (start us, length us, event | category | flops | bytes accessed | tf_op | source)
XLA Modules:
  0.0 308.2 jit_solution(1758452299170405827)
XLA Ops:
  2.1 7.3 %all-to-all-start = ((s32[8,1,128]{2,1,0:T(1,128)}), s32[8,1,128]{2,1,0:T(1,128)S(1)}, u32[]{:S(2)}, u32[]{:S(2)}) async-start(s32[8,1,128]{2,1,0:T(1,128)} %reshape.172), calls=%async_computation | async-start | bytes 8192 | tf_op jit(solution)/shard_map/all_to_all | solution.py:52
  9.4 6.6 %copy.58 = bf16[8,256,1152]{1,2,0:T(8,128)(2,1)} copy(bf16[8,256,1152]{2,1,0:T(8,128)(2,1)} %param.15) | data formatting | bytes 9437184 | tf_op jit(solution)/shard_map/while | solution.py:34
  16.6 27.6 %while.30 = (s32[]{:T(128)}, f32[8,9,8,16]{3,0,1,2:T(8,128)S(1)}, s32[]{:T(128)}, bf16[8,256]{1,0:T(8,128)(2,1)}, bf16[8,256,1152]{1,2,0:T(8,128)(2,1)}, /*index=5*/s32[]{:T(128)}, s32[]{:T(128)}, s32[]{:T(128)}) while((s32[]{:T(128)}, f32[8,9,8,16]{3,0,1,2:T(8,128)S(1)}, s32[]{:T(128)}, bf16[8,256]{1,0:T(8,128)(2,1)}, ...), condition=%wide.region_1.2_spmd, body=%wide.region_0.1_spmd.sunk | while | flops 589829 | bytes 1793675 | solution.py:34
  17.2 1.1 constant_dynamic-slice_fusion.8
  18.3 1.5 fusion.52
  20.6 1.1 constant_dynamic-slice_fusion.8
  21.7 1.5 fusion.52
  24.0 1.1 constant_dynamic-slice_fusion.8
  25.1 1.5 fusion.52
  27.3 1.1 constant_dynamic-slice_fusion.8
  28.5 1.5 fusion.52
  30.7 1.1 constant_dynamic-slice_fusion.8
  31.8 1.5 fusion.52
  34.1 1.1 constant_dynamic-slice_fusion.8
  35.2 1.5 fusion.52
  37.5 1.1 constant_dynamic-slice_fusion.8
  38.6 1.5 fusion.52
  40.9 1.1 constant_dynamic-slice_fusion.8
  42.0 1.5 fusion.52
  45.0 6.0 %all-to-all-start.1 = ((f32[8,1,1152]{2,1,0:T(1,128)}), f32[8,1,1152]{2,1,0:T(1,128)S(1)}, u32[]{:S(2)}, u32[]{:S(2)}) async-start(f32[8,1,1152]{2,1,0:T(1,128)} %reshape.174), calls=%async_computation.1 | async-start | bytes 73728 | tf_op jit(solution)/shard_map/all_to_all | solution.py:78
  52.5 5.2 %all-to-all-done.1 = f32[8,1,1152]{2,1,0:T(1,128)S(1)} async-done(((f32[8,1,1152]{2,1,0:T(1,128)}), f32[8,1,1152]{2,1,0:T(1,128)S(1)}, u32[]{:S(2)}, u32[]{:S(2)}) %all-to-all-start.1) | async-done | bytes 36896 | tf_op jit(solution)/shard_map/all_to_all | solution.py:78
  59.7 6.2 %scatter_custom_fusion = f32[9,1024]{0,1:T(8,128)S(1)} fusion(s32[1024]{0:T(1024)S(1)} %bitcast.208, f32[1024,9]{1,0:T(8,128)S(1)} %copy.61, f32[]{:T(128)} %constant.63.clone.1), kind=kCustom, calls=%fused_computation.54 | custom fusion | flops 9216 | bytes 36868 | tf_op jit(solution)/shard_map/scatter-add | solution.py:81
  65.9 16.0 %psum.49 = f32[9,1024]{0,1:T(8,128)S(1)} all-reduce(f32[9,1024]{0,1:T(8,128)S(1)} %scatter_custom_fusion), channel_id=1, replica_groups=mesh['scene'=8,'image'=4] {'image'}, use_global_device_ids=true, to_apply=%region_3.4 | all-reduce | flops 9216 | bytes 73728 | tf_op jit(solution)/shard_map/psum | solution.py:83
  82.9 3.2 %gather_fusion = bf16[1024,9]{1,0:T(8,128)(2,1)S(1)} fusion(bf16[9,1024]{0,1:T(8,128)(2,1)S(1)} %bitcast.187, s32[1024]{0:T(1024)S(1)} %broadcast_clamp_fusion), kind=kCustom, calls=%fused_computation.clone | custom fusion | bytes 40960 | tf_op jit(solution)/shard_map/jit(_take)/gather | solution.py:95
  87.4 3.3 %all-to-all-start.2 = ((bf16[8,2,576]{2,1,0:T(2,128)(2,1)}), bf16[8,2,576]{2,1,0:T(2,128)(2,1)S(1)}, u32[]{:S(2)}, u32[]{:S(2)}) async-start(bf16[8,2,576]{2,1,0:T(2,128)(2,1)} %reshape.176), calls=%async_computation.2 | async-start | bytes 40960 | tf_op jit(solution)/shard_map/all_to_all | solution.py:96
  90.7 6.5 %all-to-all-done.2 = bf16[8,2,576]{2,1,0:T(2,128)(2,1)S(1)} async-done(((bf16[8,2,576]{2,1,0:T(2,128)(2,1)}), bf16[8,2,576]{2,1,0:T(2,128)(2,1)S(1)}, u32[]{:S(2)}, u32[]{:S(2)}) %all-to-all-start.2) | async-done | bytes 18464 | tf_op jit(solution)/shard_map/all_to_all | solution.py:96
  97.6 32.4 %while.31 = (s32[]{:T(128)}, f32[8,9,8,16]{3,0,1,2:T(8,128)S(1)}, s32[]{:T(128)}, bf16[8,256,1152]{1,2,0:T(8,128)(2,1)}, bf16[8,1152]{1,0:T(8,128)(2,1)S(1)}, /*index=5*/s32[]{:T(128)}, s32[]{:T(128)}, s32[]{:T(128)}) while((s32[]{:T(128)}, f32[8,9,8,16]{3,0,1,2:T(8,128)S(1)}, s32[]{:T(128)}, bf16[8,256,1152]{1,2,0:T(8,128)(2,1)}, ...), condition=%wide.region_7.9_spmd, body=%wide.region_6.8_spmd.sunk | while | flops 1179909 | bytes 2392199 | solution.py:34
  99.3 1.2 fusion.57
  103.3 1.2 fusion.57
  107.3 1.2 fusion.57
  111.3 1.2 fusion.57
  115.2 1.2 fusion.57
  119.2 1.2 fusion.57
  123.2 1.2 fusion.57
  127.2 1.2 fusion.57
  130.2 9.1 %all_to_all.30 = f32[8,1,1152]{2,1,0:T(1,128)S(1)} all-to-all(f32[8,1,1152]{2,1,0:T(1,128)S(1)} %reshape.178), channel_id=1, replica_groups=mesh['scene'=8,'image'=4] {'scene'}, dimensions={0} | all-to-all | bytes 73728 | tf_op jit(solution)/shard_map/all_to_all | solution.py:78
  140.7 6.2 %scatter_custom_fusion.1 = f32[9,1024]{0,1:T(8,128)S(1)} fusion(s32[1024]{0:T(1024)S(1)} %bitcast.209, f32[1024,9]{1,0:T(8,128)S(1)} %copy.68, f32[]{:T(128)} %constant.63.clone.1), kind=kCustom, calls=%fused_computation.52 | custom fusion | flops 9216 | bytes 36868 | tf_op jit(solution)/shard_map/scatter-add | solution.py:81
  146.8 16.0 %psum.51 = f32[9,1024]{0,1:T(8,128)S(1)} all-reduce(f32[9,1024]{0,1:T(8,128)S(1)} %scatter_custom_fusion.1), channel_id=1, replica_groups=mesh['scene'=8,'image'=4] {'image'}, use_global_device_ids=true, to_apply=%region_9.11 | all-reduce | flops 9216 | bytes 73728 | tf_op jit(solution)/shard_map/psum | solution.py:83
  164.0 18.4 %all-reduce = (f32[]{:T(128)}, f32[]{:T(128)}) all-reduce(f32[]{:T(128)} %get-tuple-element.151, f32[]{:T(128)} %get-tuple-element.150), channel_id=1, replica_groups=mesh['scene'=8,'image'=4] {'scene'}, use_global_device_ids=true, to_apply=%region_5.6 | all-reduce | flops 2 | bytes 16 | tf_op jit(solution)/shard_map/psum | solution.py:86
  183.8 1.4 multiply_reduce_fusion.1
  185.2 19.3 %psum.53 = f32[]{:T(128)} all-reduce(f32[]{:T(128)} %get-tuple-element.184), channel_id=1, replica_groups=mesh['scene'=8,'image'=4] {'scene'}, use_global_device_ids=true, to_apply=%region_13.15 | all-reduce | flops 1 | bytes 8 | tf_op jit(solution)/shard_map/psum | solution.py:86
  206.4 3.2 %gather_fusion.1 = bf16[1024,9]{1,0:T(8,128)(2,1)S(1)} fusion(bf16[9,1024]{0,1:T(8,128)(2,1)S(1)} %bitcast.186, s32[1024]{0:T(1024)S(1)} %broadcast_clamp_fusion), kind=kCustom, calls=%fused_computation.1.clone | custom fusion | bytes 40960 | tf_op jit(solution)/shard_map/jit(_take)/gather | solution.py:95
  210.9 3.3 %all-to-all-start.4 = ((bf16[8,2,576]{2,1,0:T(2,128)(2,1)}), bf16[8,2,576]{2,1,0:T(2,128)(2,1)S(1)}, u32[]{:S(2)}, u32[]{:S(2)}) async-start(bf16[8,2,576]{2,1,0:T(2,128)(2,1)} %reshape.180), calls=%async_computation.4 | async-start | bytes 40960 | tf_op jit(solution)/shard_map/all_to_all | solution.py:96
  214.3 6.5 %all-to-all-done.4 = bf16[8,2,576]{2,1,0:T(2,128)(2,1)S(1)} async-done(((bf16[8,2,576]{2,1,0:T(2,128)(2,1)}), bf16[8,2,576]{2,1,0:T(2,128)(2,1)S(1)}, u32[]{:S(2)}, u32[]{:S(2)}) %all-to-all-start.4) | async-done | bytes 18464 | tf_op jit(solution)/shard_map/all_to_all | solution.py:96
  221.2 32.4 %while.32 = (s32[]{:T(128)}, f32[8,9,8,16]{3,0,1,2:T(8,128)S(1)}, s32[]{:T(128)}, bf16[8,256,1152]{1,2,0:T(8,128)(2,1)}, bf16[8,1152]{1,0:T(8,128)(2,1)S(1)}, /*index=5*/s32[]{:T(128)}, s32[]{:T(128)}, s32[]{:T(128)}) while((s32[]{:T(128)}, f32[8,9,8,16]{3,0,1,2:T(8,128)S(1)}, s32[]{:T(128)}, bf16[8,256,1152]{1,2,0:T(8,128)(2,1)}, ...), condition=%wide.region_15.17_spmd, body=%wide.region_14.16_spmd.sunk | while | flops 1179909 | bytes 2392199 | solution.py:34
  221.7 1.1 constant_dynamic-slice_fusion.10
  222.9 1.2 fusion.63
  225.7 1.1 constant_dynamic-slice_fusion.10
  226.8 1.2 fusion.63
  229.7 1.1 constant_dynamic-slice_fusion.10
  230.8 1.2 fusion.63
  233.7 1.1 constant_dynamic-slice_fusion.10
  234.8 1.2 fusion.63
  237.7 1.1 constant_dynamic-slice_fusion.10
  238.8 1.2 fusion.63
  242.8 1.2 fusion.63
  245.6 1.1 constant_dynamic-slice_fusion.10
  246.7 1.2 fusion.63
  249.6 1.1 constant_dynamic-slice_fusion.10
  250.7 1.2 fusion.63
  253.7 9.1 %all_to_all.31 = f32[8,1,1152]{2,1,0:T(1,128)S(1)} all-to-all(f32[8,1,1152]{2,1,0:T(1,128)S(1)} %reshape.182), channel_id=1, replica_groups=mesh['scene'=8,'image'=4] {'scene'}, dimensions={0} | all-to-all | bytes 73728 | tf_op jit(solution)/shard_map/all_to_all | solution.py:78
  264.2 6.1 %scatter_custom_fusion.2 = f32[9,1024]{0,1:T(8,128)S(1)} fusion(s32[1024]{0:T(1024)S(1)} %bitcast.210, f32[1024,9]{1,0:T(8,128)S(1)} %copy.75, f32[]{:T(128)} %constant.63.clone.1), kind=kCustom, calls=%fused_computation.50 | custom fusion | flops 9216 | bytes 36868 | tf_op jit(solution)/shard_map/scatter-add | solution.py:81
  270.4 16.0 %psum.54 = f32[9,1024]{0,1:T(8,128)S(1)} all-reduce(f32[9,1024]{0,1:T(8,128)S(1)} %scatter_custom_fusion.2), channel_id=1, replica_groups=mesh['scene'=8,'image'=4] {'image'}, use_global_device_ids=true, to_apply=%region_17.19 | all-reduce | flops 9216 | bytes 73728 | tf_op jit(solution)/shard_map/psum | solution.py:83
  287.5 18.4 %psum.55 = f32[]{:T(128)} all-reduce(f32[]{:T(128)} %multiply_reduce_fusion), channel_id=1, replica_groups=mesh['scene'=8,'image'=4] {'scene'}, use_global_device_ids=true, to_apply=%region_19.21 | all-reduce | flops 1 | bytes 8 | tf_op jit(solution)/shard_map/psum | solution.py:100
  (183 shorter events, 45.4 us)
Async XLA Ops:
  2.1 43.0 %all-to-all-start = ((s32[8,1,128]{2,1,0:T(1,128)}), s32[8,1,128]{2,1,0:T(1,128)S(1)}, u32[]{:S(2)}, u32[]{:S(2)}) async-start(s32[8,1,128]{2,1,0:T(1,128)} %reshape.172), calls=%async_computation | async-start | bytes 8192 | tf_op jit(solution)/shard_map/all_to_all | solution.py:52
  9.4 6.7 %copy-start.4 = (s32[32]{0:T(128)S(1)}, s32[32]{0:T(128)}, u32[]{:S(2)}) copy-start(s32[32]{0:T(128)} %param.18) | copy-start | bytes 388
  45.0 12.7 %all-to-all-start.1 = ((f32[8,1,1152]{2,1,0:T(1,128)}), f32[8,1,1152]{2,1,0:T(1,128)S(1)}, u32[]{:S(2)}, u32[]{:S(2)}) async-start(f32[8,1,1152]{2,1,0:T(1,128)} %reshape.174), calls=%async_computation.1 | async-start | bytes 73728 | tf_op jit(solution)/shard_map/all_to_all | solution.py:78
  52.5 29.5 %copy-start = (bf16[9,59,1024]{2,1,0:T(8,128)(2,1)S(1)}, bf16[9,59,1024]{2,1,0:T(8,128)(2,1)}, u32[]{:S(2)}) copy-start(bf16[9,59,1024]{2,1,0:T(8,128)(2,1)} %param.19) | copy-start | bytes 3262468
  59.3 23.1 %copy-start.2 = (f32[59,1024]{1,0:T(8,128)S(1)}, f32[59,1024]{1,0:T(8,128)}, u32[]{:S(2)}) copy-start(f32[59,1024]{1,0:T(8,128)} %param.21) | copy-start | bytes 724996
  87.4 9.9 %all-to-all-start.2 = ((bf16[8,2,576]{2,1,0:T(2,128)(2,1)}), bf16[8,2,576]{2,1,0:T(2,128)(2,1)S(1)}, u32[]{:S(2)}, u32[]{:S(2)}) async-start(bf16[8,2,576]{2,1,0:T(2,128)(2,1)} %reshape.176), calls=%async_computation.2 | async-start | bytes 40960 | tf_op jit(solution)/shard_map/all_to_all | solution.py:96
  140.2 23.0 %copy-start.1 = (f32[59,1024]{1,0:T(8,128)S(1)}, f32[59,1024]{1,0:T(8,128)}, u32[]{:S(2)}) copy-start(f32[59,1024]{1,0:T(8,128)} %param.20) | copy-start | bytes 724996
  210.9 9.9 %all-to-all-start.4 = ((bf16[8,2,576]{2,1,0:T(2,128)(2,1)}), bf16[8,2,576]{2,1,0:T(2,128)(2,1)S(1)}, u32[]{:S(2)}, u32[]{:S(2)}) async-start(bf16[8,2,576]{2,1,0:T(2,128)(2,1)} %reshape.180), calls=%async_computation.4 | async-start | bytes 40960 | tf_op jit(solution)/shard_map/all_to_all | solution.py:96
  264.2 43.1 %copy-start.3 = (f32[59,1024]{1,0:T(8,128)S(1)}, f32[59,1024]{1,0:T(8,128)}, u32[]{:S(2)}) copy-start(f32[59,1024]{1,0:T(8,128)} %get-tuple-element.186) | copy-start | bytes 724996
where the time goes:
time: 311 us; the launch traced here: 308 us
  blocking collectives  122 us (39%)
  local copies, waits for them, and re-layouts  55.8 us (18%)
  matrix products  44.3 us (14%)
  other arithmetic  26.6 us (9%)
  starting transfers between devices  20 us (6%)
  waiting for transfers between devices  18.3 us (6%)
  loops' own time  15.7 us (5%)
  between operations  5.17 us (2%)
    psum x3, blocking collectives, back_project(): return lax.psum(partial_sum, 'image')  48.1 us
    psum x2, blocking collectives, norm_dot(): return lax.psum(jnp.sum(residual * precon_res), 'scene')  37.7 us
    dynamic_slice x24, local copies, waits for them, and re-layouts, advance(): jac_block = lax.dynamic_index_in_dim(jac_set, position, 0, keepdims=False)  26.6 us
    dot_general x24, matrix products, advance(): returned = jnp.dot(signal, jac_block, preferred_element_type=jnp.float32)  24.4 us
    dot_general x16, matrix products, advance(): jnp.dot(jac_block, picker(position), preferred_element_type=jnp.float32)  19.8 us
    scatter-add x3, other arithmetic, back_project(): jnp.zeros((n_proj, g_dev), jnp.float32).at[:, local_ids.reshape(-1)]  18.5 us
    psum x1, blocking collectives, local(): alpha = rz_now / lax.psum(jnp.sum(direction * image), 'scene')  18.4 us
    all_to_all x2, blocking collectives, back_project(): lax.all_to_all(buffer, 'scene', split_axis=2, concat_axis=2, tiled=True)  18.2 us
  transfers between devices with their start and end apart: 4, of which 3 were waited for; matrix products, arithmetic and copies ran while one was open for 10% of the time, Pallas kernels for 0%

commit v1 on v0

--- a/solution.py
+++ b/solution.py
@@ -4,6 +4,12 @@
 from jax.sharding import PartitionSpec as P
 
 ITERS = 2
+
+
+def add_all(shard, axis):
+    pieces = lax.all_gather(shard, axis, axis=0, tiled=False)
+    total = pieces.sum(axis=0)
+    return total
 
 
 def project(proj_jac, field):
@@ -80,7 +86,7 @@
         partial_sum = (
             jnp.zeros((n_proj, g_dev), jnp.float32).at[:, local_ids.reshape(-1)].add(arrivals)
         )
-        return lax.psum(partial_sum, "image")
+        return add_all(partial_sum, "image")
 
     def norm_dot(residual, precon_res):
         return lax.psum(jnp.sum(residual * precon_res), "scene")

time: 311 us -> 280 us (0.900)
  blocking collectives: 122 us -> 91.7 us
    psum x3 -> x0, blocking collectives: 48.1 us -> none  [back_project(): return lax.psum(partial_sum, 'image')]
    all_gather x0 -> x3, blocking collectives: none -> 17.3 us  [add_all(): pieces = lax.all_gather(shard, axis, axis=0, tiled=False)]
  transfers between devices with their start and end apart: 4 -> 4, of which waited for: 3 -> 3; matrix products, arithmetic and copies ran while one was open for 10% -> 12% of each run, Pallas kernels for 0% -> 0%
where the time goes in v1:
time: 280 us; the launch traced here: 277 us
  blocking collectives  91.7 us (33%)
  local copies, waits for them, and re-layouts  55.9 us (20%)
  matrix products  44.3 us (16%)
  other arithmetic  26.1 us (9%)
  starting transfers between devices  20 us (7%)
  waiting for transfers between devices  18.3 us (7%)
  loops' own time  15.7 us (6%)
  between operations  5.11 us (2%)
    psum x2, blocking collectives, norm_dot(): return lax.psum(jnp.sum(residual * precon_res), 'scene')  37.8 us
    dynamic_slice x24, local copies, waits for them, and re-layouts, advance(): jac_block = lax.dynamic_index_in_dim(jac_set, position, 0, keepdims=False)  26.6 us
    dot_general x24, matrix products, advance(): returned = jnp.dot(signal, jac_block, preferred_element_type=jnp.float32)  24.4 us
    dot_general x16, matrix products, advance(): jnp.dot(jac_block, picker(position), preferred_element_type=jnp.float32)  19.9 us
    scatter-add x3, other arithmetic, back_project(): jnp.zeros((n_proj, g_dev), jnp.float32).at[:, local_ids.reshape(-1)]  18.5 us
    psum x1, blocking collectives, local(): alpha = rz_now / lax.psum(jnp.sum(direction * image), 'scene')  18.4 us
    all_to_all x2, blocking collectives, back_project(): lax.all_to_all(buffer, 'scene', split_axis=2, concat_axis=2, tiled=True)  18.2 us
    all_gather x3, blocking collectives, add_all(): pieces = lax.all_gather(shard, axis, axis=0, tiled=False)  17.3 us
  transfers between devices with their start and end apart: 4, of which 3 were waited for; matrix products, arithmetic and copies ran while one was open for 12% of the time, Pallas kernels for 0%

profile of v1, /device:TPU:0, one launch (start us, length us, event | category | flops | bytes accessed | tf_op | source)
XLA Modules:
  0.0 277.1 jit_solution(5634760982652337878)
XLA Ops:
  2.1 7.3 %all-to-all-start = ((s32[8,1,128]{2,1,0:T(1,128)}), s32[8,1,128]{2,1,0:T(1,128)S(1)}, u32[]{:S(2)}, u32[]{:S(2)}) async-start(s32[8,1,128]{2,1,0:T(1,128)} %reshape.184), calls=%async_computation | async-start | bytes 8192 | tf_op jit(solution)/shard_map/all_to_all | solution.py:58
  9.4 6.6 %copy.70 = bf16[8,256,1152]{1,2,0:T(8,128)(2,1)} copy(bf16[8,256,1152]{2,1,0:T(8,128)(2,1)} %param.15) | data formatting | bytes 9437184 | tf_op jit(solution)/shard_map/while | solution.py:40
  16.6 27.7 %while.30 = (s32[]{:T(128)}, f32[8,9,8,16]{3,0,1,2:T(8,128)S(1)}, s32[]{:T(128)}, bf16[8,256]{1,0:T(8,128)(2,1)}, bf16[8,256,1152]{1,2,0:T(8,128)(2,1)}, /*index=5*/s32[]{:T(128)}, s32[]{:T(128)}, s32[]{:T(128)}) while((s32[]{:T(128)}, f32[8,9,8,16]{3,0,1,2:T(8,128)S(1)}, s32[]{:T(128)}, bf16[8,256]{1,0:T(8,128)(2,1)}, ...), condition=%wide.region_1.2_spmd, body=%wide.region_0.1_spmd.sunk | while | flops 589829 | bytes 1793675 | solution.py:40
  17.2 1.1 constant_dynamic-slice_fusion.8
  18.3 1.5 fusion.52
  20.6 1.1 constant_dynamic-slice_fusion.8
  21.7 1.5 fusion.52
  24.0 1.1 constant_dynamic-slice_fusion.8
  25.1 1.5 fusion.52
  27.4 1.1 constant_dynamic-slice_fusion.8
  28.5 1.5 fusion.52
  30.8 1.1 constant_dynamic-slice_fusion.8
  31.9 1.5 fusion.52
  34.2 1.1 constant_dynamic-slice_fusion.8
  35.3 1.5 fusion.52
  37.5 1.1 constant_dynamic-slice_fusion.8
  38.7 1.5 fusion.52
  40.9 1.1 constant_dynamic-slice_fusion.8
  42.1 1.5 fusion.52
  45.1 6.0 %all-to-all-start.1 = ((f32[8,1,1152]{2,1,0:T(1,128)}), f32[8,1,1152]{2,1,0:T(1,128)S(1)}, u32[]{:S(2)}, u32[]{:S(2)}) async-start(f32[8,1,1152]{2,1,0:T(1,128)} %reshape.186), calls=%async_computation.1 | async-start | bytes 73728 | tf_op jit(solution)/shard_map/all_to_all | solution.py:84
  52.6 5.2 %all-to-all-done.1 = f32[8,1,1152]{2,1,0:T(1,128)S(1)} async-done(((f32[8,1,1152]{2,1,0:T(1,128)}), f32[8,1,1152]{2,1,0:T(1,128)S(1)}, u32[]{:S(2)}, u32[]{:S(2)}) %all-to-all-start.1) | async-done | bytes 36896 | tf_op jit(solution)/shard_map/all_to_all | solution.py:84
  59.7 6.2 %scatter_custom_fusion = f32[9,1024]{0,1:T(8,128)S(1)} fusion(s32[1024]{0:T(1024)S(1)} %bitcast.217, f32[1024,9]{1,0:T(8,128)S(1)} %copy.73, f32[]{:T(128)} %constant.63.clone.1), kind=kCustom, calls=%fused_computation.54 | custom fusion | flops 9216 | bytes 36868 | tf_op jit(solution)/shard_map/scatter-add | solution.py:87
  66.1 5.8 %all-gather.3 = f32[4,9,1024]{2,1,0:T(8,128)S(1)} all-gather(f32[1,9,1024]{2,1,0:T(8,128)S(1)} %copy.74), channel_id=2, replica_groups=mesh['scene'=8,'image'=4] {'image'}, dimensions={0}, use_global_device_ids=true | all-gather | bytes 184320 | tf_op jit(solution)/shard_map/all_gather | solution.py:10
  72.7 3.2 %gather_fusion = bf16[1024,9]{1,0:T(8,128)(2,1)S(1)} fusion(bf16[9,1024]{0,1:T(8,128)(2,1)S(1)} %bitcast.193, s32[1024]{0:T(1024)S(1)} %broadcast_clamp_fusion), kind=kCustom, calls=%fused_computation.clone | custom fusion | bytes 40960 | tf_op jit(solution)/shard_map/jit(_take)/gather | solution.py:101
  77.2 3.3 %all-to-all-start.2 = ((bf16[8,2,576]{2,1,0:T(2,128)(2,1)}), bf16[8,2,576]{2,1,0:T(2,128)(2,1)S(1)}, u32[]{:S(2)}, u32[]{:S(2)}) async-start(bf16[8,2,576]{2,1,0:T(2,128)(2,1)} %reshape.188), calls=%async_computation.2 | async-start | bytes 40960 | tf_op jit(solution)/shard_map/all_to_all | solution.py:102
  80.5 6.5 %all-to-all-done.2 = bf16[8,2,576]{2,1,0:T(2,128)(2,1)S(1)} async-done(((bf16[8,2,576]{2,1,0:T(2,128)(2,1)}), bf16[8,2,576]{2,1,0:T(2,128)(2,1)S(1)}, u32[]{:S(2)}, u32[]{:S(2)}) %all-to-all-start.2) | async-done | bytes 18464 | tf_op jit(solution)/shard_map/all_to_all | solution.py:102
  87.4 32.4 %while.31 = (s32[]{:T(128)}, f32[8,9,8,16]{3,0,1,2:T(8,128)S(1)}, s32[]{:T(128)}, bf16[8,256,1152]{1,2,0:T(8,128)(2,1)}, bf16[8,1152]{1,0:T(8,128)(2,1)S(1)}, /*index=5*/s32[]{:T(128)}, s32[]{:T(128)}, s32[]{:T(128)}) while((s32[]{:T(128)}, f32[8,9,8,16]{3,0,1,2:T(8,128)S(1)}, s32[]{:T(128)}, bf16[8,256,1152]{1,2,0:T(8,128)(2,1)}, ...), condition=%wide.region_7.9_spmd, body=%wide.region_6.8_spmd.sunk | while | flops 1179909 | bytes 2392199 | solution.py:40
  89.1 1.2 fusion.57
  93.1 1.2 fusion.57
  97.1 1.2 fusion.57
  101.1 1.2 fusion.57
  105.0 1.2 fusion.57
  109.0 1.2 fusion.57
  113.0 1.2 fusion.57
  117.0 1.2 fusion.57
  120.0 9.1 %all_to_all.30 = f32[8,1,1152]{2,1,0:T(1,128)S(1)} all-to-all(f32[8,1,1152]{2,1,0:T(1,128)S(1)} %reshape.190), channel_id=1, replica_groups=mesh['scene'=8,'image'=4] {'scene'}, dimensions={0} | all-to-all | bytes 73728 | tf_op jit(solution)/shard_map/all_to_all | solution.py:84
  130.5 6.2 %scatter_custom_fusion.1 = f32[9,1024]{0,1:T(8,128)S(1)} fusion(s32[1024]{0:T(1024)S(1)} %bitcast.218, f32[1024,9]{1,0:T(8,128)S(1)} %copy.82, f32[]{:T(128)} %constant.63.clone.1), kind=kCustom, calls=%fused_computation.52 | custom fusion | flops 9216 | bytes 36868 | tf_op jit(solution)/shard_map/scatter-add | solution.py:87
  136.9 5.8 %all-gather.4 = f32[4,9,1024]{2,1,0:T(8,128)S(1)} all-gather(f32[1,9,1024]{2,1,0:T(8,128)S(1)} %copy.83), channel_id=3, replica_groups=mesh['scene'=8,'image'=4] {'image'}, dimensions={0}, use_global_device_ids=true | all-gather | bytes 184320 | tf_op jit(solution)/shard_map/all_gather | solution.py:10
  143.7 18.5 %all-reduce = (f32[]{:T(128)}, f32[]{:T(128)}) all-reduce(f32[]{:T(128)} %get-tuple-element.151, f32[]{:T(128)} %get-tuple-element.150), channel_id=1, replica_groups=mesh['scene'=8,'image'=4] {'scene'}, use_global_device_ids=true, to_apply=%region_5.6 | all-reduce | flops 2 | bytes 16 | tf_op jit(solution)/shard_map/psum | solution.py:92
  164.3 19.3 %psum.30 = f32[]{:T(128)} all-reduce(f32[]{:T(128)} %get-tuple-element.184), channel_id=1, replica_groups=mesh['scene'=8,'image'=4] {'scene'}, use_global_device_ids=true, to_apply=%region_13.15 | all-reduce | flops 1 | bytes 8 | tf_op jit(solution)/shard_map/psum | solution.py:92
  185.5 3.2 %gather_fusion.1 = bf16[1024,9]{1,0:T(8,128)(2,1)S(1)} fusion(bf16[9,1024]{0,1:T(8,128)(2,1)S(1)} %bitcast.192, s32[1024]{0:T(1024)S(1)} %broadcast_clamp_fusion), kind=kCustom, calls=%fused_computation.1.clone | custom fusion | bytes 40960 | tf_op jit(solution)/shard_map/jit(_take)/gather | solution.py:101
  190.0 3.3 %all-to-all-start.4 = ((bf16[8,2,576]{2,1,0:T(2,128)(2,1)}), bf16[8,2,576]{2,1,0:T(2,128)(2,1)S(1)}, u32[]{:S(2)}, u32[]{:S(2)}) async-start(bf16[8,2,576]{2,1,0:T(2,128)(2,1)} %reshape.192), calls=%async_computation.4 | async-start | bytes 40960 | tf_op jit(solution)/shard_map/all_to_all | solution.py:102
  193.4 6.5 %all-to-all-done.4 = bf16[8,2,576]{2,1,0:T(2,128)(2,1)S(1)} async-done(((bf16[8,2,576]{2,1,0:T(2,128)(2,1)}), bf16[8,2,576]{2,1,0:T(2,128)(2,1)S(1)}, u32[]{:S(2)}, u32[]{:S(2)}) %all-to-all-start.4) | async-done | bytes 18464 | tf_op jit(solution)/shard_map/all_to_all | solution.py:102
  200.3 32.5 %while.32 = (s32[]{:T(128)}, f32[8,9,8,16]{3,0,1,2:T(8,128)S(1)}, s32[]{:T(128)}, bf16[8,256,1152]{1,2,0:T(8,128)(2,1)}, bf16[8,1152]{1,0:T(8,128)(2,1)S(1)}, /*index=5*/s32[]{:T(128)}, s32[]{:T(128)}, s32[]{:T(128)}) while((s32[]{:T(128)}, f32[8,9,8,16]{3,0,1,2:T(8,128)S(1)}, s32[]{:T(128)}, bf16[8,256,1152]{1,2,0:T(8,128)(2,1)}, ...), condition=%wide.region_15.17_spmd, body=%wide.region_14.16_spmd.sunk | while | flops 1179909 | bytes 2392199 | solution.py:40
  200.8 1.1 constant_dynamic-slice_fusion.10
  201.9 1.2 fusion.63
  204.8 1.1 constant_dynamic-slice_fusion.10
  205.9 1.2 fusion.63
  208.8 1.1 constant_dynamic-slice_fusion.10
  209.9 1.2 fusion.63
  212.8 1.1 constant_dynamic-slice_fusion.10
  213.9 1.2 fusion.63
  216.8 1.1 constant_dynamic-slice_fusion.10
  217.9 1.2 fusion.63
  220.8 1.1 constant_dynamic-slice_fusion.10
  221.9 1.2 fusion.63
  224.8 1.1 constant_dynamic-slice_fusion.10
  225.9 1.2 fusion.63
  228.7 1.1 constant_dynamic-slice_fusion.10
  229.9 1.2 fusion.63
  232.9 9.1 %all_to_all.31 = f32[8,1,1152]{2,1,0:T(1,128)S(1)} all-to-all(f32[8,1,1152]{2,1,0:T(1,128)S(1)} %reshape.194), channel_id=1, replica_groups=mesh['scene'=8,'image'=4] {'scene'}, dimensions={0} | all-to-all | bytes 73728 | tf_op jit(solution)/shard_map/all_to_all | solution.py:84
  243.3 6.2 %scatter_custom_fusion.2 = f32[9,1024]{0,1:T(8,128)S(1)} fusion(s32[1024]{0:T(1024)S(1)} %bitcast.219, f32[1024,9]{1,0:T(8,128)S(1)} %copy.91, f32[]{:T(128)} %constant.63.clone.1), kind=kCustom, calls=%fused_computation.50 | custom fusion | flops 9216 | bytes 36868 | tf_op jit(solution)/shard_map/scatter-add | solution.py:87
  249.7 5.8 %all-gather.5 = f32[4,9,1024]{2,1,0:T(8,128)S(1)} all-gather(f32[1,9,1024]{2,1,0:T(8,128)S(1)} %copy.92), channel_id=4, replica_groups=mesh['scene'=8,'image'=4] {'image'}, dimensions={0}, use_global_device_ids=true | all-gather | bytes 184320 | tf_op jit(solution)/shard_map/all_gather | solution.py:10
  256.4 18.4 %psum.31 = f32[]{:T(128)} all-reduce(f32[]{:T(128)} %multiply_reduce_fusion), channel_id=1, replica_groups=mesh['scene'=8,'image'=4] {'scene'}, use_global_device_ids=true, to_apply=%region_19.21 | all-reduce | flops 1 | bytes 8 | tf_op jit(solution)/shard_map/psum | solution.py:106
  (184 shorter events, 45.3 us)
Async XLA Ops:
  2.1 43.0 %all-to-all-start = ((s32[8,1,128]{2,1,0:T(1,128)}), s32[8,1,128]{2,1,0:T(1,128)S(1)}, u32[]{:S(2)}, u32[]{:S(2)}) async-start(s32[8,1,128]{2,1,0:T(1,128)} %reshape.184), calls=%async_computation | async-start | bytes 8192 | tf_op jit(solution)/shard_map/all_to_all | solution.py:58
  9.4 6.7 %copy-start.3 = (s32[32]{0:T(128)S(1)}, s32[32]{0:T(128)}, u32[]{:S(2)}) copy-start(s32[32]{0:T(128)} %param.18) | copy-start | bytes 388
  45.1 12.7 %all-to-all-start.1 = ((f32[8,1,1152]{2,1,0:T(1,128)}), f32[8,1,1152]{2,1,0:T(1,128)S(1)}, u32[]{:S(2)}, u32[]{:S(2)}) async-start(f32[8,1,1152]{2,1,0:T(1,128)} %reshape.186), calls=%async_computation.1 | async-start | bytes 73728 | tf_op jit(solution)/shard_map/all_to_all | solution.py:84
  52.3 19.6 %copy-start = (bf16[9,59,1024]{2,1,0:T(8,128)(2,1)S(1)}, bf16[9,59,1024]{2,1,0:T(8,128)(2,1)}, u32[]{:S(2)}) copy-start(bf16[9,59,1024]{2,1,0:T(8,128)(2,1)} %param.19) | copy-start | bytes 3262468
  59.2 12.9 %copy-start.2 = (f32[59,1024]{1,0:T(8,128)S(1)}, f32[59,1024]{1,0:T(8,128)}, u32[]{:S(2)}) copy-start(f32[59,1024]{1,0:T(8,128)} %param.21) | copy-start | bytes 724996
  77.2 9.9 %all-to-all-start.2 = ((bf16[8,2,576]{2,1,0:T(2,128)(2,1)}), bf16[8,2,576]{2,1,0:T(2,128)(2,1)S(1)}, u32[]{:S(2)}, u32[]{:S(2)}) async-start(bf16[8,2,576]{2,1,0:T(2,128)(2,1)} %reshape.188), calls=%async_computation.2 | async-start | bytes 40960 | tf_op jit(solution)/shard_map/all_to_all | solution.py:102
  130.0 12.9 %copy-start.1 = (f32[59,1024]{1,0:T(8,128)S(1)}, f32[59,1024]{1,0:T(8,128)}, u32[]{:S(2)}) copy-start(f32[59,1024]{1,0:T(8,128)} %param.20) | copy-start | bytes 724996
  190.0 9.9 %all-to-all-start.4 = ((bf16[8,2,576]{2,1,0:T(2,128)(2,1)}), bf16[8,2,576]{2,1,0:T(2,128)(2,1)S(1)}, u32[]{:S(2)}, u32[]{:S(2)}) async-start(bf16[8,2,576]{2,1,0:T(2,128)(2,1)} %reshape.192), calls=%async_computation.4 | async-start | bytes 40960 | tf_op jit(solution)/shard_map/all_to_all | solution.py:102
